TPU v7x, 32 devices: a whole 2x2x4 slice. The times are simulated.
32 devices in a mesh: seq: 8 (over z, x), stream: 4 (over y, core).
Axes of the slice: x: 2, y: 2, z: 4, core: 2. Of those that a mesh axis runs over, the one named last changes fastest.
Arguments:
- tokens: bfloat16 [4, 4096, 768], P('stream', 'seq'), may hold values from -6 to 6
- segment_ids: int32 [4, 4096], P('stream', 'seq'), may hold values from -1 to 32, as said below
- query_key_value_weight: bfloat16 [768, 2304], replicated, may hold values from -0.21875 to 0.21875
- conv_kernel: bfloat16 [3, 2304], replicated, may hold values from -3 to 3
- attention_output_weight: bfloat16 [768, 768], replicated, may hold values from -0.875 to 0.875
- up_weight: bfloat16 [768, 3072], replicated, may hold values from -0.21875 to 0.21875
- down_weight: bfloat16 [3072, 768], replicated, may hold values from -0.109375 to 0.109375
- gain_attn: bfloat16 [768], replicated, may hold values from 0.5 to 1.5
- shift_attn: bfloat16 [768], replicated, may hold values from -3 to 3
- gain_ffn: bfloat16 [768], replicated, may hold values from 0.5 to 1.5
- shift_ffn: bfloat16 [768], replicated, may hold values from -3 to 3
- cotangent: bfloat16 [4, 4096, 768], P('stream', 'seq'), may hold values from -6 to 6
Outputs:
- out_tokens: bfloat16 [4, 4096, 768], P('stream', 'seq')
- grad_tokens: float32 [4, 4096, 768], P('stream', 'seq')
- grad_w_qkv: float32 [768, 2304], replicated
- grad_conv_kernel: float32 [3, 2304], replicated
- grad_w_out: float32 [768, 768], replicated
- grad_w_up: float32 [768, 3072], replicated
- grad_w_down: float32 [3072, 768], replicated
- grad_gain_attn: float32 [768], replicated
- grad_shift_attn: float32 [768], replicated
- grad_gain_ffn: float32 [768], replicated
- grad_shift_ffn: float32 [768], replicated
Inputs may be any that keep to these rules, and one draw needn't show every extreme that they name: `segment_ids`: along each pack the document numbers never fall and differ between documents; each document fills 128 to 256 consecutive slots, one of 256 slots in every pack; the last document of every pack has the number 4096 // 128; slots between documents hold -1, and so does the last slot of each pack.
All inputs are finite; a program needn't handle non-finite values.
Results may differ from a plain program's by a relative error of at most 0.019.
Values may be sent and summed in bfloat16 or wider, within the bound.
No kernel may reach another device: no remote copies, remote signals or barrier semaphores. Data moves between devices by JAX's collectives and lax.ppermute only.
A program may use at most 256 MiB of HBM per device.

v0:
```python
import math
import jax
import jax.numpy as jnp
from jax import lax
from jax.sharding import PartitionSpec as P

H = 12
HD = 64
EPSILON = 1e-05
MASKED = -1e30


def passed_along(block, axis, distance):
    devices = range(lax.axis_size(axis))
    route = [(i - distance, i) for i in devices if i - distance in devices]
    return lax.ppermute(block, axis, route)


def layer_norm(field, gain, shift):
    center = field - jnp.mean(field, -1, keepdims=True)
    spread = jnp.mean(center * center, -1, keepdims=True)
    return center * lax.rsqrt(spread + EPSILON) * gain + shift


def square_relu(field):
    return jnp.square(jnp.maximum(field, 0.0))


def conv_local(extended, kernel, same_one, same_two):
    row_count = extended.shape[1] - 2
    result = kernel[0] * extended[:, 2:]
    result = result + kernel[1] * extended[:, 1 : row_count + 1] * same_one
    result = result + kernel[2] * extended[:, :row_count] * same_two
    return result


def pair_scores(queries, key_rows, query_ids, key_ids, query_pos, key_pos):
    raw_scores = jnp.einsum(
        "sqhd,skhd->shqk", queries, key_rows, preferred_element_type=jnp.float32
    )
    allowed = (query_ids[:, :, None] == key_ids[:, None, :]) & (key_ids[:, None, :] >= 0)
    allowed = (
        allowed
        & (key_pos[None, None, :] <= query_pos[None, :, None])
        & (key_pos[None, None, :] >= 0)
    )
    allowed = allowed | (key_pos[None, None, :] == query_pos[None, :, None])
    return jnp.where(allowed[:, None], raw_scores * (1.0 / math.sqrt(HD)), MASKED)


def on_device(
    tokens,
    segment_ids,
    query_key_value_weight,
    conv_kernel,
    attention_output_weight,
    up_weight,
    down_weight,
    gain_attn,
    shift_attn,
    gain_ffn,
    shift_ffn,
    cotangent,
):
    pack_count, slot_count, model_width = tokens.shape
    device_at = lax.axis_index("seq")
    slot_steps = jnp.arange(slot_count, dtype=jnp.int32)
    query_pos = device_at * slot_count + slot_steps
    own_live = segment_ids >= 0
    active_token_mask = own_live.astype(jnp.float32)[..., None]
    inputs = tokens.astype(jnp.float32)
    normalized_first, norm_one_back = jax.vjp(
        layer_norm, inputs, gain_attn.astype(jnp.float32), shift_attn.astype(jnp.float32)
    )
    normalized_first_narrow = normalized_first.astype(jnp.bfloat16)
    mixed_query_key_value = jnp.einsum(
        "jmc,ct->jmt",
        normalized_first_narrow,
        query_key_value_weight,
        preferred_element_type=jnp.float32,
    )
    halo_rows, halo_ids = passed_along(
        (mixed_query_key_value[:, -2:], segment_ids[:, -2:]), "seq", 1
    )
    extended = jnp.concatenate([halo_rows, mixed_query_key_value], 1)
    extended_ids = jnp.concatenate([halo_ids, segment_ids], 1)
    same_one = ((extended_ids[:, 1 : slot_count + 1] == segment_ids) & own_live).astype(
        jnp.float32
    )[..., None]
    same_two = ((extended_ids[:, :slot_count] == segment_ids) & own_live).astype(jnp.float32)[
        ..., None
    ]
    convolved, conv_back = jax.vjp(
        lambda field, weights: conv_local(field, weights, same_one, same_two),
        extended,
        conv_kernel.astype(jnp.float32),
    )
    conv_low = convolved.astype(jnp.bfloat16)
    head_shape = (pack_count, slot_count, H, HD)
    queries = conv_low[..., :model_width].reshape(head_shape)
    pair_kv = conv_low[..., model_width:]
    prior_kv, prior_ids = passed_along((pair_kv, segment_ids), "seq", 1)
    shard_kv = jnp.stack([prior_kv, pair_kv])
    shard_ids = jnp.stack([prior_ids, segment_ids])
    shard_at = device_at - 1 + jnp.arange(2, dtype=jnp.int32)
    shard_total = shard_kv.shape[0]
    first_id = jnp.min(jnp.where(own_live, segment_ids, 1 << 30))

    def shard_view(shard):
        block_kv = lax.dynamic_index_in_dim(shard_kv, shard, 0, keepdims=False)
        key_rows = block_kv[..., :model_width].reshape(head_shape)
        value_rows = block_kv[..., model_width:].reshape(head_shape)
        key_ids = lax.dynamic_index_in_dim(shard_ids, shard, 0, keepdims=False)
        owner = lax.dynamic_index_in_dim(shard_at, shard, 0, keepdims=False)
        key_pos = owner * slot_count + slot_steps
        useful = (owner == device_at) | (owner < device_at) & (owner >= 0) & (
            jnp.max(key_ids) >= first_id
        )
        return (key_rows, value_rows, key_ids, key_pos, useful)

    def keep_state(state):
        return state

    def top_step(shard, state):
        key_rows, value_rows, key_ids, key_pos, useful = shard_view(shard)

        def top_work(inner):
            row_top, row_total = inner
            scores = pair_scores(queries, key_rows, segment_ids, key_ids, query_pos, key_pos)
            new_top = jnp.maximum(row_top, jnp.max(scores, -1))
            row_total = row_total * jnp.exp(row_top - new_top) + jnp.sum(
                jnp.exp(scores - new_top[..., None]), -1
            )
            return (new_top, row_total)

        return lax.cond(useful, top_work, keep_state, state)

    stat_shape = (pack_count, H, slot_count)
    row_top, row_total = lax.fori_loop(
        0,
        shard_total,
        top_step,
        (jnp.full(stat_shape, MASKED, jnp.float32), jnp.zeros(stat_shape, jnp.float32)),
    )
    log_total = row_top + jnp.log(row_total)

    def probs_for(key_rows, key_ids, key_pos):
        scores = pair_scores(queries, key_rows, segment_ids, key_ids, query_pos, key_pos)
        return jnp.exp(scores - log_total[..., None])

    def out_step(shard, state):
        key_rows, value_rows, key_ids, key_pos, useful = shard_view(shard)

        def out_work(inner):
            probs = probs_for(key_rows, key_ids, key_pos)
            return inner + jnp.einsum(
                "shqk,skhd->sqhd",
                probs.astype(jnp.bfloat16),
                value_rows,
                preferred_element_type=jnp.float32,
            )

        return lax.cond(useful, out_work, keep_state, state)

    attention_result = lax.fori_loop(0, shard_total, out_step, jnp.zeros(head_shape, jnp.float32))
    attention_result = attention_result.reshape(pack_count, slot_count, model_width).astype(
        jnp.bfloat16
    )
    residual_branch = jnp.einsum(
        "jmc,ct->jmt", attention_result, attention_output_weight, preferred_element_type=jnp.float32
    )
    middle_state = inputs + active_token_mask * residual_branch
    normalized_second, norm_two_back = jax.vjp(
        layer_norm, middle_state, gain_ffn.astype(jnp.float32), shift_ffn.astype(jnp.float32)
    )
    normalized_second_narrow = normalized_second.astype(jnp.bfloat16)
    hidden_state = jnp.einsum(
        "zha,ay->zhy", normalized_second_narrow, up_weight, preferred_element_type=jnp.float32
    )
    activated_hidden, relu_back = jax.vjp(square_relu, hidden_state)
    activated_narrow = activated_hidden.astype(jnp.bfloat16)
    feedforward_output = jnp.einsum(
        "nxg,gi->nxi", activated_narrow, down_weight, preferred_element_type=jnp.float32
    )
    out_tokens = (middle_state + active_token_mask * feedforward_output).astype(jnp.bfloat16)
    grad_out = cotangent.astype(jnp.float32)
    gradient_residual_branch = (active_token_mask * grad_out).astype(jnp.bfloat16)
    grad_w_down = jnp.einsum(
        "ipr,iph->rh",
        activated_narrow,
        gradient_residual_branch,
        preferred_element_type=jnp.float32,
    )
    gradient_activated = jnp.einsum(
        "owr,ar->owa", gradient_residual_branch, down_weight, preferred_element_type=jnp.float32
    )
    gradient_hidden_state = relu_back(gradient_activated)[0].astype(jnp.bfloat16)
    grad_w_up = jnp.einsum(
        "jtw,jth->wh",
        normalized_second_narrow,
        gradient_hidden_state,
        preferred_element_type=jnp.float32,
    )
    grad_normed_two = jnp.einsum(
        "ytw,pw->ytp", gradient_hidden_state, up_weight, preferred_element_type=jnp.float32
    )
    grad_middle_part, grad_gain_ffn, grad_shift_ffn = norm_two_back(grad_normed_two)
    grad_middle = grad_out + grad_middle_part
    gradient_attention_branch = (active_token_mask * grad_middle).astype(jnp.bfloat16)
    grad_w_out = jnp.einsum(
        "tir,tiv->rv",
        attention_result,
        gradient_attention_branch,
        preferred_element_type=jnp.float32,
    )
    grad_heads = (
        jnp.einsum(
            "tig,ag->tia",
            gradient_attention_branch,
            attention_output_weight,
            preferred_element_type=jnp.float32,
        )
        .astype(jnp.bfloat16)
        .reshape(head_shape)
    )

    def delta_step(shard, state):
        key_rows, value_rows, key_ids, key_pos, useful = shard_view(shard)

        def delta_work(inner):
            probs = probs_for(key_rows, key_ids, key_pos)
            grad_probs = jnp.einsum(
                "sqhd,skhd->shqk", grad_heads, value_rows, preferred_element_type=jnp.float32
            )
            return inner + jnp.sum(probs * grad_probs, -1)

        return lax.cond(useful, delta_work, keep_state, state)

    row_delta = lax.fori_loop(0, shard_total, delta_step, jnp.zeros(stat_shape, jnp.float32))

    def grad_step(shard, state):
        key_rows, value_rows, key_ids, key_pos, useful = shard_view(shard)

        def grad_work(inner):
            grad_queries, key_terms = inner
            probs = probs_for(key_rows, key_ids, key_pos)
            grad_probs = jnp.einsum(
                "sqhd,skhd->shqk", grad_heads, value_rows, preferred_element_type=jnp.float32
            )
            grad_scores = (
                probs * (grad_probs - row_delta[..., None]) * (1.0 / math.sqrt(HD))
            ).astype(jnp.bfloat16)
            grad_queries = grad_queries + jnp.einsum(
                "shqk,skhd->sqhd", grad_scores, key_rows, preferred_element_type=jnp.float32
            )
            grad_keys = jnp.einsum(
                "shqk,sqhd->skhd", grad_scores, queries, preferred_element_type=jnp.float32
            )
            grad_values = jnp.einsum(
                "shqk,sqhd->skhd",
                probs.astype(jnp.bfloat16),
                grad_heads,
                preferred_element_type=jnp.float32,
            )
            key_piece = jnp.concatenate(
                [
                    grad_keys.reshape(pack_count, slot_count, model_width),
                    grad_values.reshape(pack_count, slot_count, model_width),
                ],
                -1,
            )
            key_terms = lax.dynamic_update_index_in_dim(key_terms, key_piece, shard, 0)
            return (grad_queries, key_terms)

        return lax.cond(useful, grad_work, keep_state, state)

    term_init = jnp.zeros((shard_total, pack_count, slot_count, 2 * model_width), jnp.float32)
    grad_queries, key_terms = lax.fori_loop(
        0, shard_total, grad_step, (jnp.zeros(head_shape, jnp.float32), term_init)
    )
    grad_kv = key_terms[1] + passed_along(key_terms[0].astype(jnp.bfloat16), "seq", -1).astype(
        jnp.float32
    )
    grad_conv = jnp.concatenate(
        [grad_queries.reshape(pack_count, slot_count, model_width), grad_kv], -1
    )
    grad_extended, grad_kernel = conv_back(grad_conv)
    back_rows = passed_along(grad_extended[:, :2], "seq", -1)
    gradient_mixed_projection = grad_extended[:, 2:]
    gradient_mixed_projection = jnp.concatenate(
        [gradient_mixed_projection[:, :-2], gradient_mixed_projection[:, -2:] + back_rows], 1
    ).astype(jnp.bfloat16)
    grad_w_qkv = jnp.einsum(
        "tir,tiv->rv",
        normalized_first_narrow,
        gradient_mixed_projection,
        preferred_element_type=jnp.float32,
    )
    gradient_normalized_first = jnp.einsum(
        "tig,ag->tia",
        gradient_mixed_projection,
        query_key_value_weight,
        preferred_element_type=jnp.float32,
    )
    grad_input_part, grad_gain_attn, grad_shift_attn = norm_one_back(gradient_normalized_first)
    grad_tokens = grad_middle + grad_input_part
    grads = [
        grad_w_qkv,
        grad_kernel,
        grad_w_out,
        grad_w_up,
        grad_w_down,
        grad_gain_attn,
        grad_shift_attn,
        grad_gain_ffn,
        grad_shift_ffn,
    ]
    flat = jnp.concatenate([piece.reshape(-1) for piece in grads])
    shares = lax.psum_scatter(
        flat.astype(jnp.bfloat16), "seq", scatter_dimension=0, tiled=True
    ).astype(jnp.float32)
    shares = lax.psum(shares.astype(jnp.bfloat16), "stream").astype(jnp.float32)
    summed = lax.all_gather(shares.astype(jnp.bfloat16), "seq", axis=0, tiled=True).astype(
        shares.dtype
    )
    results = []
    offset = 0
    for piece in grads:
        count = piece.size
        results.append(summed[offset : offset + count].reshape(piece.shape))
        offset = offset + count
    return (
        out_tokens,
        grad_tokens,
        results[0],
        results[1],
        results[2],
        results[3],
        results[4],
        results[5],
        results[6],
        results[7],
        results[8],
    )


def solution(mesh):
    return jax.shard_map(
        on_device,
        mesh=mesh,
        in_specs=(
            P("stream", "seq", None),
            P("stream", "seq"),
            P(),
            P(),
            P(),
            P(),
            P(),
            P(),
            P(),
            P(),
            P(),
            P("stream", "seq", None),
        ),
        out_specs=(
            P("stream", "seq", None),
            P("stream", "seq", None),
            P(),
            P(),
            P(),
            P(),
            P(),
            P(),
            P(),
            P(),
            P(),
        ),
        check_vma=False,
    )
```

profile of v0, /device:TPU:0, one launch (start us, length us, event | category | flops | bytes accessed | tf_op | source)
XLA Modules:
  0.0 1588.4 jit_solution(7274010136364462006)
XLA Ops:
  41.8 25.5 %collective-permute-done = s32[1,512]{1,0:T(1,128)S(1)} collective-permute-done((s32[1,512]{1,0:T(1,128)S(1)}, s32[1,512]{1,0:T(1,128)S(1)}, u32[]{:S(2)}, u32[]{:S(2)}) %collective-permute-start) | collective-permute-done | bytes 2080 | tf_op jit(solution)/shard_map/ppermute | solution.py:16
  81.4 21.0 %while.66 = (s32[]{:T(128)}, f32[1,12,512]{2,1,0:T(8,128)}, f32[1,12,512]{2,1,0:T(8,128)}, s32[2]{0:T(128)}, s32[]{:T(128)}, /*index=5*/s32[2,1,512]{2,1,0:T(1,1...) while((s32[]{:T(128)}, f32[1,12,512]{2,1,0:T(8,128)}, ...), condition=%wide.region_9.10_spmd.clone, body=%wide.region_3.9_spmd.clone.sunk | while | flops 426523136 | bytes 36882872 | solution.py:139
  91.6 10.8 conditional.12
  105.1 23.4 %while.67 = (s32[]{:T(128)}, f32[1,512,12,64]{1,3,2,0:T(8,128)}, s32[2]{0:T(128)}, s32[]{:T(128)}, s32[2,1,512]{2,1,0:T(1,128)S(1)}, /*index=5*/s32[]{:T(128)}, ...) while((s32[]{:T(128)}, f32[1,512,12,64]{1,3,2,0:T(8,128)}, ...), condition=%wide.region_14.15_spmd.clone, body=%wide.region_10.14_spmd.clone.sunk | while | flops 820120064 | bytes 12372291 | solution.py:165
  115.8 12.2 conditional.13
  120.6 7.4 bitcast_add_fusion.1
  150.8 21.0 %while.68 = (s32[]{:T(128)}, f32[1,12,512]{2,1,0:T(8,128)}, s32[2]{0:T(128)}, s32[]{:T(128)}, s32[2,1,512]{2,1,0:T(1,128)S(1)}, /*index=5*/s32[]{:T(128)}, s32[1...) while((s32[]{:T(128)}, f32[1,12,512]{2,1,0:T(8,128)}, ...), condition=%wide.region_24.25_spmd.clone, body=%wide.region_19.24_spmd.clone.sunk | while | flops 822872576 | bytes 41666984 | solution.py:239
  161.2 10.5 conditional.14
  176.6 41.2 %while.69 = (s32[]{:T(128)}, f32[1,512,12,64]{1,3,2,0:T(8,128)}, f32[2,1,512,1536]{2,3,1,0:T(8,128)}, s32[2]{0:T(128)}, s32[]{:T(128)}, /*index=5*/s32[2,1,512]{...) while((s32[]{:T(128)}, f32[1,512,12,64]{1,3,2,0:T(8,128)}, ...), condition=%wide.region_29.30_spmd.clone, body=%wide.region_25.29_spmd.clone.sunk | while | flops 2050886144 | bytes 144902832 | solution.py:278
  187.7 30.1 %conditional.15 = ((f32[1,512,12,64]{1,3,2,0:T(8,128)}, f32[2,1,512,1536]{2,3,1,0:T(8,128)})) conditional(s32[]{:T(128)} %convert_element_type.256, (f32[1,512,12,64]{1,3,2,0:T(8,128)}, f32[2,1,512,1536]{2,3,1,0:T(8,128)}) %tuple.244, (bf16[2,1,512,1536]{2,3,1,0:T(8,128)(2,1)}, s32[]{:T(128)}, s32[1,512]{1,0:T(1,128)S(1)}, ...), branch_computations={%region_27.27_spmd, %region_28.28_spmd} | conditional | flops 2050885632 | bytes 144896320 | solution.py:275
  190.8 6.4 fusion.52
  197.2 6.1 fusion.44
  203.4 7.3 fusion.40
  217.8 6.6 copy.66
  228.9 7.9 convolution_convert_fusion
  236.7 9.4 reshape.1646
  268.4 59.5 %collective-permute-done.4 = bf16[1,512,1536]{2,1,0:T(8,128)(2,1)} collective-permute-done((bf16[1,512,1536]{2,1,0:T(8,128)(2,1)}, bf16[1,512,1536]{2,1,0:T(8,128)(2,1)}, u32[]{:S(2)}, u32[]{:S(2)}) %collective-permute-start.4) | collective-permute-done | bytes 1572896 | tf_op jit(solution)/shard_map/ppermute | solution.py:16
  330.7 6.3 multiply_reduce_fusion.1
  356.0 6.1 collective-permute-done.5
  376.2 7.7 reshape.1642
  388.7 19.2 %dynamic-update-slice.3 = bf16[7087872]{0:T(1024)(128)(2,1)} dynamic-update-slice(bf16[7087872]{0:T(1024)(128)(2,1)} %dynamic-update-slice.2, bf16[589824]{0:T(1024)(128)(2,1)} %reshape.1644, s32[]{} %constant.348) | dynamic-update-slice | bytes 2359300
  407.9 72.5 %dynamic-update-slice.4 = bf16[7087872]{0:T(1024)(128)(2,1)} dynamic-update-slice(bf16[7087872]{0:T(1024)(128)(2,1)} %dynamic-update-slice.3, bf16[2359296]{0:T(1024)(128)(2,1)} %bitcast.265, s32[]{} %constant.349) | dynamic-update-slice | bytes 9437188
  480.5 72.4 %dynamic-update-slice.5 = bf16[7087872]{0:T(1024)(128)(2,1)} dynamic-update-slice(bf16[7087872]{0:T(1024)(128)(2,1)} %dynamic-update-slice.4, bf16[2359296]{0:T(1024)(128)(2,1)} %reshape.1646, s32[]{} %constant.350) | dynamic-update-slice | bytes 9437188
  559.5 444.2 %all-reduce.16.cloned.1.call-done = bf16[7087872]{0:T(1024)(128)(2,1)} async-done(((bf16[7087872]{0:T(1024)(128)(2,1)}), bf16[7087872]{0:T(1024)(128)(2,1)}) %all-reduce.16.cloned.1.call-update) | async-done | bytes 14175760
  1008.2 44.8 %all-reduce.12.cloned.1.call-done = bf16[885984]{0:T(1024)(128)(2,1)} async-done(((bf16[885984]{0:T(1024)(128)(2,1)}), bf16[885984]{0:T(1024)(128)(2,1)}) %all-reduce.12.cloned.1.call-update) | async-done | bytes 1771984 | tf_op jit(solution)/shard_map/psum | solution.py:322
  1058.1 28.2 %dynamic-update-slice = bf16[7087872]{0:T(1024)(128)(2,1)} dynamic-update-slice(bf16[7087872]{0:T(1024)(128)(2,1)} %broadcast.947, bf16[885984]{0:T(1024)(128)(2,1)} %all-reduce.12.cloned.1.call-done, u32[]{:T(128)} %bitcast.83) | dynamic-update-slice | bytes 3543940
  1087.0 8.4 fusion.78
  1097.4 428.8 %all-reduce.14.cloned.1.call-done = bf16[7087872]{0:T(1024)(128)(2,1)} async-done(((bf16[7087872]{0:T(1024)(128)(2,1)}), bf16[7087872]{0:T(1024)(128)(2,1)}) %all-reduce.14.cloned.1.call-update) | async-done | bytes 14175760
  1539.9 8.2 reshape.1647
  1548.1 10.0 fusion.112
  1558.1 11.3 slice.198
  1569.4 10.9 reshape.1649
  (354 shorter events, 226.9 us)
Async XLA Ops:
  7.2 10.2 copy-start
  7.2 996.4 %all-reduce.16.cloned.1.call-start = ((), (), s32[]{:S(2)}) async-start(), calls=%async_computation.2 | async-start | bytes 28352512
  8.1 16.2 %collective-permute-start.2 = (s32[1,2]{1,0:T(1,128)S(1)}, s32[1,2]{1,0:T(1,128)S(1)}, u32[]{:S(2)}, u32[]{:S(2)}) collective-permute-start(s32[1,2]{1,0:T(1,128)S(1)} %slice.180), channel_id=1, source_target_pairs={{0,4},{4,8},{8,12},{12,16},{16,20},{20,24},{24,28},{1,5},{5,9},{9,... | collective-permute-start | bytes 32 | tf_op jit(solution)/shard_map/ppermute | solution.py:16
  20.7 4.9 collective-permute-start.1
  28.1 12.5 copy-start.80
  28.1 13.1 copy-start.81
  30.6 41.1 %collective-permute-start.3 = (bf16[1,512,1536]{2,1,0:T(8,128)(2,1)}, bf16[1,512,1536]{2,1,0:T(8,128)(2,1)}, u32[]{:S(2)}, u32[]{:S(2)}) collective-permute-start(bf16[1,512,1536]{2,1,0:T(8,128)(2,1)} %get-tuple-element.1763), channel_id=1, source_target_pairs={{0,4},{4,8},{8,12},{12,16},{16,20},{20,24},{24,28},{1,5},{5,9},{9,... | collective-permute-start | bytes 4718600 | tf_op jit(solution)/shard_map/ppermute | solution.py:16
  35.9 31.4 %collective-permute-start = (s32[1,512]{1,0:T(1,128)S(1)}, s32[1,512]{1,0:T(1,128)S(1)}, u32[]{:S(2)}, u32[]{:S(2)}) collective-permute-start(s32[1,512]{1,0:T(1,128)S(1)} %copy-done.27), channel_id=1, source_target_pairs={{0,4},{4,8},{8,12},{12,16},{16,20},{20,24},{24,28},{1,5},{5,9},{9,... | collective-permute-start | bytes 6152 | tf_op jit(solution)/shard_map/ppermute | solution.py:16
  132.8 10.1 copy-start.20
  132.9 10.1 copy-start.56
  133.3 9.6 copy-start.70
  217.8 11.1 copy-start.68
  227.6 100.3 %collective-permute-start.4 = (bf16[1,512,1536]{2,1,0:T(8,128)(2,1)}, bf16[1,512,1536]{2,1,0:T(8,128)(2,1)}, u32[]{:S(2)}, u32[]{:S(2)}) collective-permute-start(bf16[1,512,1536]{2,1,0:T(8,128)(2,1)} %fusion.75), channel_id=1, source_target_pairs={{4,0},{8,4},{12,8},{16,12},{20,16},{24,20},{28,24},{5,1},{9,5},{13... | collective-permute-start | bytes 4718600 | tf_op jit(solution)/shard_map/ppermute | solution.py:16
  236.7 11.5 copy-start.57
  236.7 11.5 copy-start.66
  236.7 11.5 copy-start.71
  236.7 11.5 copy-start.79
  268.4 62.3 %copy-start.22 = (f32[1,512,768]{2,1,0:T(8,128)S(1)}, f32[1,512,768]{2,1,0:T(8,128)}, u32[]{:S(2)}) copy-start(f32[1,512,768]{2,1,0:T(8,128)} %copy.68) | copy-start | bytes 4718596
  268.4 62.3 %copy-start.35 = (f32[2304]{0:T(1024)S(1)}, f32[2304]{0:T(1024)}, u32[]{:S(2)}) copy-start(f32[2304]{0:T(1024)} %copy-done.34) | copy-start | bytes 27652
  268.4 62.3 %copy-start.37 = (f32[2304]{0:T(1024)S(1)}, f32[2304]{0:T(1024)}, u32[]{:S(2)}) copy-start(f32[2304]{0:T(1024)} %copy-done.36) | copy-start | bytes 27652
  268.4 62.3 %copy-start.39 = (f32[2304]{0:T(1024)S(1)}, f32[2304]{0:T(1024)}, u32[]{:S(2)}) copy-start(f32[2304]{0:T(1024)} %copy-done.38) | copy-start | bytes 27652
  268.4 62.3 %copy-start.41 = (f32[1,2,2304]{2,1,0:T(2,128)S(1)}, f32[1,2,2304]{2,1,0:T(2,128)}, u32[]{:S(2)}) copy-start(f32[1,2,2304]{2,1,0:T(2,128)} %copy-done.40) | copy-start | bytes 55300
  268.4 62.3 %copy-start.62 = (f32[1,512]{1,0:T(1,128)S(1)}, f32[1,512]{1,0:T(1,128)}, u32[]{:S(2)}) copy-start(f32[1,512]{1,0:T(1,128)} %copy-done.61) | copy-start | bytes 6148
  268.4 62.3 %copy-start.64 = (f32[1,512]{1,0:T(1,128)S(1)}, f32[1,512]{1,0:T(1,128)}, u32[]{:S(2)}) copy-start(f32[1,512]{1,0:T(1,128)} %copy-done.63) | copy-start | bytes 6148
  351.0 11.2 collective-permute-start.5
  480.4 72.4 %copy-start.75 = (bf16[768]{0:T(1024)(128)(2,1)S(1)}, bf16[768]{0:T(1024)(128)(2,1)}, u32[]{:S(2)}) copy-start(bf16[768]{0:T(1024)(128)(2,1)} %get-tuple-element.1627) | copy-start | bytes 4612
  480.4 73.8 %copy-start.74 = (bf16[768]{0:T(1024)(128)(2,1)S(1)}, bf16[768]{0:T(1024)(128)(2,1)}, u32[]{:S(2)}) copy-start(bf16[768]{0:T(1024)(128)(2,1)} %reduce_sum.178) | copy-start | bytes 4612
  480.4 75.2 %copy-start.83 = (bf16[768]{0:T(1024)(128)(2,1)S(1)}, bf16[768]{0:T(1024)(128)(2,1)}, u32[]{:S(2)}) copy-start(bf16[768]{0:T(1024)(128)(2,1)} %get-tuple-element.1625) | copy-start | bytes 4612
  480.4 76.5 %copy-start.72 = (bf16[768]{0:T(1024)(128)(2,1)S(1)}, bf16[768]{0:T(1024)(128)(2,1)}, u32[]{:S(2)}) copy-start(bf16[768]{0:T(1024)(128)(2,1)} %reduce_sum.183) | copy-start | bytes 4612
  557.6 495.4 %all-reduce.12.cloned.1.call-start = ((), (), s32[]{:S(2)}) async-start(), calls=%async_computation | async-start | bytes 3547136 | tf_op jit(solution)/shard_map/psum | solution.py:322
  1007.3 518.9 %all-reduce.14.cloned.1.call-start = ((), (), s32[]{:S(2)}) async-start(), calls=%async_computation.1 | async-start | bytes 28352512
  1087.0 8.5 copy-start.25
  (71 other events, 305.3 us)
Sparse Core Ops, SparseCore 0:
  557.7 445.8 all-reduce.15
  1007.4 45.4 all-reduce.11
  1086.5 439.7 all-reduce.13
where the time goes:
time: 1620 us; the launch traced here: 1590 us
  waiting for transfers between devices  1010 us (62%)
  local copies, waits for them, and re-layouts  363 us (22%)
  matrix products  86.2 us (5%)
  other arithmetic  62.3 us (4%)
  loops' own time  30.1 us (2%)
  starting transfers between devices  20.5 us (1%)
  between operations  16.3 us (1%)
    unnamed x5, waiting for transfers between devices  873 us
    unnamed x174, local copies, waits for them, and re-layouts  228 us
    ppermute x6, waiting for transfers between devices, passed_along(): return lax.ppermute(block, axis, route)  91.8 us
    psum x1, waiting for transfers between devices, on_device(): shares = lax.psum(shares.astype(jnp.bfloat16), 'stream').astype(jnp.float32)  44.8 us
    slice x7, local copies, waits for them, and re-layouts, on_device(): results.append(summed[offset:offset + count].reshape(piece.shape))  34.9 us
  transfers between devices with their start and end apart: 9, of which 7 were waited for; matrix products, arithmetic and copies ran while one was open for 4% of the time, Pallas kernels for 0%

commit v1 on v0

--- a/solution.py
+++ b/solution.py
@@ -319,7 +319,9 @@
     shares = lax.psum_scatter(
         flat.astype(jnp.bfloat16), "seq", scatter_dimension=0, tiled=True
     ).astype(jnp.float32)
-    shares = lax.psum(shares.astype(jnp.bfloat16), "stream").astype(jnp.float32)
+    shares = jnp.sum(lax.all_gather(shares.astype(jnp.bfloat16), "stream"), axis=0).astype(
+        jnp.float32
+    )
     summed = lax.all_gather(shares.astype(jnp.bfloat16), "seq", axis=0, tiled=True).astype(
         shares.dtype
     )

time: 1620 us -> 1780 us (1.099)
  waiting for transfers between devices: 1010 us -> 1090 us
  local copies, waits for them, and re-layouts: 363 us -> 405 us
  other arithmetic: 62.3 us -> 99.1 us
    unnamed x5 -> x6, waiting for transfers between devices: 873 us -> 1000 us
    psum x1 -> x0, waiting for transfers between devices: 44.8 us -> none  [on_device(): shares = lax.psum(shares.astype(jnp.bfloat16), 'stream').astype(jnp.float32)]
    reduce_sum x0 -> x1, other arithmetic: none -> 37.1 us  [on_device(): jnp.sum(lax.all_gather(shares.astype(jnp.bfloat16), 'stream'), axis=0)]
    unnamed x174 -> x179, local copies, waits for them, and re-layouts: 228 us -> 260 us
where the time goes in v1:
time: 1780 us; the launch traced here: 1750 us
  waiting for transfers between devices  1090 us (61%)
  local copies, waits for them, and re-layouts  405 us (23%)
  other arithmetic  99.1 us (6%)
  matrix products  86.2 us (5%)
  loops' own time  28.3 us (2%)
  starting transfers between devices  20.3 us (1%)
    unnamed x6, waiting for transfers between devices  1000 us
    unnamed x179, local copies, waits for them, and re-layouts  260 us
    ppermute x6, waiting for transfers between devices, passed_along(): return lax.ppermute(block, axis, route)  91.8 us
    reduce_sum x1, other arithmetic, on_device(): jnp.sum(lax.all_gather(shares.astype(jnp.bfloat16), 'stream'), axis=0)  37.1 us
  transfers between devices with their start and end apart: 9, of which 7 were waited for; matrix products, arithmetic and copies ran while one was open for 4% of the time, Pallas kernels for 0%

profile of v1, /device:TPU:0, one launch (start us, length us, event | category | flops | bytes accessed | tf_op | source)
XLA Modules:
  0.0 1751.1 jit_solution(10227578031631669933)
XLA Ops:
  41.8 25.4 %collective-permute-done = s32[1,512]{1,0:T(1,128)S(1)} collective-permute-done((s32[1,512]{1,0:T(1,128)S(1)}, s32[1,512]{1,0:T(1,128)S(1)}, u32[]{:S(2)}, u32[]{:S(2)}) %collective-permute-start) | collective-permute-done | bytes 2080 | tf_op jit(solution)/shard_map/ppermute | solution.py:16
  81.4 20.8 %while.66 = (s32[]{:T(128)}, f32[1,12,512]{2,1,0:T(8,128)}, f32[1,12,512]{2,1,0:T(8,128)}, s32[2]{0:T(128)}, s32[]{:T(128)}, /*index=5*/s32[2,1,512]{2,1,0:T(1,1...) while((s32[]{:T(128)}, f32[1,12,512]{2,1,0:T(8,128)}, ...), condition=%wide.region_9.10_spmd.clone, body=%wide.region_3.9_spmd.clone.sunk | while | flops 426523136 | bytes 36882872 | solution.py:139
  91.4 10.8 conditional.12
  104.9 22.3 %while.67 = (s32[]{:T(128)}, f32[1,512,12,64]{1,3,2,0:T(8,128)}, s32[2]{0:T(128)}, s32[]{:T(128)}, s32[2,1,512]{2,1,0:T(1,128)S(1)}, /*index=5*/s32[]{:T(128)}, ...) while((s32[]{:T(128)}, f32[1,512,12,64]{1,3,2,0:T(8,128)}, ...), condition=%wide.region_14.15_spmd.clone, body=%wide.region_10.14_spmd.clone.sunk | while | flops 820120064 | bytes 12372291 | solution.py:165
  115.0 12.2 conditional.13
  119.7 7.4 bitcast_add_fusion.1
  149.5 20.5 %while.68 = (s32[]{:T(128)}, f32[1,12,512]{2,1,0:T(8,128)}, s32[2]{0:T(128)}, s32[]{:T(128)}, s32[2,1,512]{2,1,0:T(1,128)S(1)}, /*index=5*/s32[]{:T(128)}, s32[1...) while((s32[]{:T(128)}, f32[1,12,512]{2,1,0:T(8,128)}, ...), condition=%wide.region_24.25_spmd.clone, body=%wide.region_19.24_spmd.clone.sunk | while | flops 822872576 | bytes 41666984 | solution.py:239
  159.5 10.5 conditional.14
  174.9 40.2 %while.69 = (s32[]{:T(128)}, f32[1,512,12,64]{1,3,2,0:T(8,128)}, f32[2,1,512,1536]{2,3,1,0:T(8,128)}, s32[2]{0:T(128)}, s32[]{:T(128)}, /*index=5*/s32[2,1,512]{...) while((s32[]{:T(128)}, f32[1,512,12,64]{1,3,2,0:T(8,128)}, ...), condition=%wide.region_29.30_spmd.clone, body=%wide.region_25.29_spmd.clone.sunk | while | flops 2050886144 | bytes 144902832 | solution.py:278
  185.0 30.0 %conditional.15 = ((f32[1,512,12,64]{1,3,2,0:T(8,128)}, f32[2,1,512,1536]{2,3,1,0:T(8,128)})) conditional(s32[]{:T(128)} %convert_element_type.258, (f32[1,512,12,64]{1,3,2,0:T(8,128)}, f32[2,1,512,1536]{2,3,1,0:T(8,128)}) %tuple.248, (bf16[2,1,512,1536]{2,3,1,0:T(8,128)(2,1)}, s32[]{:T(128)}, s32[1,512]{1,0:T(1,128)S(1)}, ...), branch_computations={%region_27.27_spmd, %region_28.28_spmd} | conditional | flops 2050885632 | bytes 144896320 | solution.py:275
  200.7 7.3 fusion.40
  215.1 6.6 copy.81
  226.1 7.9 convolution_convert_fusion
  234.0 9.6 reshape.1646
  265.9 59.0 %collective-permute-done.4 = bf16[1,512,1536]{2,1,0:T(8,128)(2,1)} collective-permute-done((bf16[1,512,1536]{2,1,0:T(8,128)(2,1)}, bf16[1,512,1536]{2,1,0:T(8,128)(2,1)}, u32[]{:S(2)}, u32[]{:S(2)}) %collective-permute-start.4) | collective-permute-done | bytes 1572896 | tf_op jit(solution)/shard_map/ppermute | solution.py:16
  352.9 6.6 collective-permute-done.5
  373.5 7.7 reshape.1642
  386.0 19.2 %dynamic-update-slice.4 = bf16[7087872]{0:T(1024)(128)(2,1)} dynamic-update-slice(bf16[7087872]{0:T(1024)(128)(2,1)} %dynamic-update-slice.3, bf16[589824]{0:T(1024)(128)(2,1)} %reshape.1644, s32[]{} %constant.356) | dynamic-update-slice | bytes 2359300
  405.2 72.4 %dynamic-update-slice.5 = bf16[7087872]{0:T(1024)(128)(2,1)} dynamic-update-slice(bf16[7087872]{0:T(1024)(128)(2,1)} %dynamic-update-slice.4, bf16[2359296]{0:T(1024)(128)(2,1)} %bitcast.266, s32[]{} %constant.357) | dynamic-update-slice | bytes 9437188
  477.7 72.4 %dynamic-update-slice.6 = bf16[7087872]{0:T(1024)(128)(2,1)} dynamic-update-slice(bf16[7087872]{0:T(1024)(128)(2,1)} %dynamic-update-slice.5, bf16[2359296]{0:T(1024)(128)(2,1)} %reshape.1646, s32[]{} %constant.358) | dynamic-update-slice | bytes 9437188
  557.9 442.7 %all-reduce.17.cloned.1.call-done = bf16[7087872]{0:T(1024)(128)(2,1)} async-done(((bf16[7087872]{0:T(1024)(128)(2,1)}), bf16[7087872]{0:T(1024)(128)(2,1)}) %all-reduce.17.cloned.1.call-update) | async-done | bytes 14175760
  1007.5 28.3 %dynamic-update-slice = bf16[3543936]{0:T(1024)(128)(2,1)} dynamic-update-slice(bf16[3543936]{0:T(1024)(128)(2,1)} %broadcast.947, bf16[885984]{0:T(1024)(128)(2,1)} %dynamic-slice.3, u32[]{:T(128)} %bitcast.83) | dynamic-update-slice | bytes 3543940
  1036.4 131.3 %all-reduce.13.cloned.1.call-done = bf16[3543936]{0:T(1024)(128)(2,1)} async-done(((bf16[3543936]{0:T(1024)(128)(2,1)}), bf16[3543936]{0:T(1024)(128)(2,1)}) %all-reduce.13.cloned.1.call-update) | async-done | bytes 7087888
  1167.8 10.7 reshape.1653
  1178.5 37.1 %reduce_sum.198 = bf16[885984]{0:T(1024)(128)(2,1)} reduce(bf16[4,885984]{1,0:T(4,128)(2,1)} %reshape.1653, bf16[]{:T(256)} %constant.314.clone.1), dimensions={0}, to_apply=%region_40.41 | reduce | flops 2657952 | bytes 8859842 | tf_op jit(solution)/shard_map/reduce_sum | solution.py:322
  1220.7 28.2 %dynamic-update-slice.1 = bf16[7087872]{0:T(1024)(128)(2,1)} dynamic-update-slice(bf16[7087872]{0:T(1024)(128)(2,1)} %broadcast.948, bf16[885984]{0:T(1024)(128)(2,1)} %reduce_sum.198, u32[]{:T(128)} %bitcast.84) | dynamic-update-slice | bytes 3543940
  1249.7 8.4 fusion.78
  1260.0 428.9 %all-reduce.15.cloned.1.call-done = bf16[7087872]{0:T(1024)(128)(2,1)} async-done(((bf16[7087872]{0:T(1024)(128)(2,1)}), bf16[7087872]{0:T(1024)(128)(2,1)}) %all-reduce.15.cloned.1.call-update) | async-done | bytes 14175760
  1702.5 8.2 reshape.1647
  1710.7 10.1 fusion.112
  1720.8 11.3 slice.198
  1732.1 10.9 reshape.1649
  (361 shorter events, 248.2 us)
Async XLA Ops:
  7.2 10.2 copy-start
  7.2 993.4 %all-reduce.17.cloned.1.call-start = ((), (), s32[]{:S(2)}) async-start(), calls=%async_computation.2 | async-start | bytes 28352512
  8.1 16.2 collective-permute-start.2
  20.7 4.9 collective-permute-start.1
  28.1 12.5 copy-start.80
  28.1 13.1 copy-start.81
  30.6 41.1 %collective-permute-start.3 = (bf16[1,512,1536]{2,1,0:T(8,128)(2,1)}, bf16[1,512,1536]{2,1,0:T(8,128)(2,1)}, u32[]{:S(2)}, u32[]{:S(2)}) collective-permute-start(bf16[1,512,1536]{2,1,0:T(8,128)(2,1)} %get-tuple-element.1811), channel_id=1, source_target_pairs={{0,4},{4,8},{8,12},{12,16},{16,20},{20,24},{24,28},{1,5},{5,9},{9,... | collective-permute-start | bytes 4718600 | tf_op jit(solution)/shard_map/ppermute | solution.py:16
  35.9 31.4 %collective-permute-start = (s32[1,512]{1,0:T(1,128)S(1)}, s32[1,512]{1,0:T(1,128)S(1)}, u32[]{:S(2)}, u32[]{:S(2)}) collective-permute-start(s32[1,512]{1,0:T(1,128)S(1)} %copy-done.27), channel_id=1, source_target_pairs={{0,4},{4,8},{8,12},{12,16},{16,20},{20,24},{24,28},{1,5},{5,9},{9,... | collective-permute-start | bytes 6152 | tf_op jit(solution)/shard_map/ppermute | solution.py:16
  131.6 10.1 copy-start.20
  131.6 10.1 copy-start.56
  132.1 9.6 copy-start.70
  215.1 11.1 copy-start.68
  224.8 100.1 %collective-permute-start.4 = (bf16[1,512,1536]{2,1,0:T(8,128)(2,1)}, bf16[1,512,1536]{2,1,0:T(8,128)(2,1)}, u32[]{:S(2)}, u32[]{:S(2)}) collective-permute-start(bf16[1,512,1536]{2,1,0:T(8,128)(2,1)} %fusion.75), channel_id=1, source_target_pairs={{4,0},{8,4},{12,8},{16,12},{20,16},{24,20},{28,24},{5,1},{9,5},{13... | collective-permute-start | bytes 4718600 | tf_op jit(solution)/shard_map/ppermute | solution.py:16
  234.0 11.7 copy-start.57
  234.0 11.7 copy-start.66
  234.0 11.7 copy-start.71
  234.0 11.7 copy-start.79
  265.9 61.9 %copy-start.22 = (f32[1,512,768]{2,1,0:T(8,128)S(1)}, f32[1,512,768]{2,1,0:T(8,128)}, u32[]{:S(2)}) copy-start(f32[1,512,768]{2,1,0:T(8,128)} %copy.83) | copy-start | bytes 4718596
  265.9 61.9 %copy-start.35 = (f32[2304]{0:T(1024)S(1)}, f32[2304]{0:T(1024)}, u32[]{:S(2)}) copy-start(f32[2304]{0:T(1024)} %copy-done.34) | copy-start | bytes 27652
  265.9 61.9 %copy-start.37 = (f32[2304]{0:T(1024)S(1)}, f32[2304]{0:T(1024)}, u32[]{:S(2)}) copy-start(f32[2304]{0:T(1024)} %copy-done.36) | copy-start | bytes 27652
  265.9 61.9 %copy-start.39 = (f32[2304]{0:T(1024)S(1)}, f32[2304]{0:T(1024)}, u32[]{:S(2)}) copy-start(f32[2304]{0:T(1024)} %copy-done.38) | copy-start | bytes 27652
  265.9 61.9 %copy-start.41 = (f32[1,2,2304]{2,1,0:T(2,128)S(1)}, f32[1,2,2304]{2,1,0:T(2,128)}, u32[]{:S(2)}) copy-start(f32[1,2,2304]{2,1,0:T(2,128)} %copy-done.40) | copy-start | bytes 55300
  265.9 61.9 %copy-start.62 = (f32[1,512]{1,0:T(1,128)S(1)}, f32[1,512]{1,0:T(1,128)}, u32[]{:S(2)}) copy-start(f32[1,512]{1,0:T(1,128)} %copy-done.61) | copy-start | bytes 6148
  265.9 61.9 %copy-start.64 = (f32[1,512]{1,0:T(1,128)S(1)}, f32[1,512]{1,0:T(1,128)}, u32[]{:S(2)}) copy-start(f32[1,512]{1,0:T(1,128)} %copy-done.63) | copy-start | bytes 6148
  336.3 8.5 slice-start
  348.0 11.4 collective-permute-start.5
  477.7 72.4 %copy-start.75 = (bf16[768]{0:T(1024)(128)(2,1)S(1)}, bf16[768]{0:T(1024)(128)(2,1)}, u32[]{:S(2)}) copy-start(bf16[768]{0:T(1024)(128)(2,1)} %get-tuple-element.1675) | copy-start | bytes 4612
  477.7 73.8 %copy-start.74 = (bf16[768]{0:T(1024)(128)(2,1)S(1)}, bf16[768]{0:T(1024)(128)(2,1)}, u32[]{:S(2)}) copy-start(bf16[768]{0:T(1024)(128)(2,1)} %reduce_sum.192) | copy-start | bytes 4612
  477.7 75.1 %copy-start.83 = (bf16[768]{0:T(1024)(128)(2,1)S(1)}, bf16[768]{0:T(1024)(128)(2,1)}, u32[]{:S(2)}) copy-start(bf16[768]{0:T(1024)(128)(2,1)} %get-tuple-element.1673) | copy-start | bytes 4612
  477.7 76.5 %copy-start.73 = (bf16[768]{0:T(1024)(128)(2,1)S(1)}, bf16[768]{0:T(1024)(128)(2,1)}, u32[]{:S(2)}) copy-start(bf16[768]{0:T(1024)(128)(2,1)} %reduce_sum.197) | copy-start | bytes 4612
  554.8 613.0 %all-reduce.13.cloned.1.call-start = ((), (), s32[]{:S(2)}) async-start(), calls=%async_computation | async-start | bytes 14176256
  1035.7 653.2 %all-reduce.15.cloned.1.call-start = ((), (), s32[]{:S(2)}) async-start(), calls=%async_computation.1 | async-start | bytes 28352512
  (72 other events, 308.3 us)
Sparse Core Ops, SparseCore 0:
  554.9 445.6 all-reduce.16
  1035.9 131.8 all-reduce.12
  1249.1 439.7 all-reduce.14
